TPU v7x, 32 devices: a whole 2x2x4 slice. The times are simulated.
32 devices in a mesh: work: 8 (over z, y), firm: 4 (over x, core).
Axes of the slice: x: 2, y: 2, z: 4, core: 2. Of those that a mesh axis runs over, the one named last changes fastest.
Arguments:
- worker_feat: bfloat16 [64, 16384], P('firm', 'work'), may hold values from -4 to 4
- firm_feat: bfloat16 [64, 16384], P('work', 'firm'), may hold values from -1.75 to 1.75
- worker_pot: float32 [16384], P('work'), may hold values from -1 to 1
- firm_pot: float32 [16384], P('firm'), may hold values from -1 to 1
- worker_caps: int32 [16384], P('work'), may hold values from 1 to 5
- firm_caps: int32 [16384], P('firm'), may hold values from 1 to 5
Outputs:
- step_workers: float32 [16384], P('work')
- step_firms: float32 [16384], P('firm')
All inputs are finite; a program needn't handle non-finite values.
Results may differ from a plain program's by a relative error of at most 0.0003.
Values may be sent and summed in bfloat16 or wider, within the bound.
A program may use at most 64 MiB of HBM per device.

v0:
```python
import math
import jax
import jax.numpy as jnp
from jax import lax
from jax.sharding import PartitionSpec as P

ITERS = 4


def body(worker_feat, firm_feat, worker_pot, firm_pot, worker_caps, firm_caps):
    wfeat = lax.all_gather(worker_feat, "firm", axis=0, tiled=True)
    ffeat = lax.all_gather(firm_feat, "work", axis=0, tiled=True)
    rows_here = wfeat.shape[1]
    cols_here = ffeat.shape[1]
    inverse = 1.0 / (cols_here * lax.axis_size("firm"))
    scale = 1.0 / math.sqrt(wfeat.shape[0])
    width = 256
    blocks = cols_here // width
    first_firm = lax.axis_index("firm") == 0
    first_work = lax.axis_index("work") == 0

    def kernel_pass(vec_u, vec_v):

        def step(rows_acc, index):
            start = index * width
            feat_blk = lax.dynamic_slice_in_dim(ffeat, start, width, 1)
            pot_blk = lax.dynamic_slice_in_dim(firm_pot, start, width, 0)
            vec_blk = lax.dynamic_slice_in_dim(vec_v, start, width, 0)
            surplus = lax.dot_general(
                wfeat, feat_blk, (((0,), (0,)), ((), ())), preferred_element_type=jnp.float32
            )
            kernel = jnp.exp(surplus * scale - worker_pot[:, None] - pot_blk[None, :]) * inverse
            rows_acc = rows_acc + jnp.dot(kernel, vec_blk, precision=lax.Precision.HIGHEST)
            col_blk = jnp.dot(vec_u, kernel, precision=lax.Precision.HIGHEST)
            return (rows_acc, col_blk)

        rows_part, col_blocks = lax.scan(
            step, jnp.zeros((rows_here,), jnp.float32), jnp.arange(blocks, dtype=jnp.int32)
        )
        rows_full = lax.psum(rows_part, "firm")
        cols_part = col_blocks.reshape(cols_here)
        cols = lax.psum(cols_part, "work")
        return (rows_full, cols)

    row_total, col_total = kernel_pass(
        jnp.ones((rows_here,), jnp.float32), jnp.ones((cols_here,), jnp.float32)
    )
    diag_u = row_total + jnp.exp(-worker_pot)
    diag_v = col_total + jnp.exp(-firm_pot)
    rhs_u = diag_u - worker_caps.astype(jnp.float32)
    rhs_v = diag_v - firm_caps.astype(jnp.float32)

    def hessian(dir_u, dir_v):
        prod_u, prod_v = kernel_pass(dir_u, dir_v)
        return (diag_u * dir_u + prod_u, diag_v * dir_v + prod_v)

    def local_dot(left_u, left_v, right_u, right_v):
        part_u = jnp.where(first_firm, jnp.sum(left_u * right_u), 0.0)
        part_v = jnp.where(first_work, jnp.sum(left_v * right_v), 0.0)
        return part_u + part_v

    step_u = jnp.zeros_like(rhs_u)
    step_v = jnp.zeros_like(rhs_v)
    res_u, res_v = (rhs_u, rhs_v)

    def two_products(left_u, left_v, image_u, image_v):
        return lax.psum(
            (
                local_dot(left_u, left_v, left_u, left_v),
                local_dot(left_u, left_v, image_u, image_v),
            ),
            ("work", "firm"),
        )

    image_u, image_v = hessian(res_u, res_v)
    norm_now, product = two_products(res_u, res_v, image_u, image_v)
    alpha = norm_now / product
    dir_u, dir_v = (res_u, res_v)
    along_u, along_v = (image_u, image_v)
    for index in range(ITERS):
        step_u = step_u + alpha * dir_u
        step_v = step_v + alpha * dir_v
        if index + 1 < ITERS:
            res_u = res_u - alpha * along_u
            res_v = res_v - alpha * along_v
            image_u, image_v = hessian(res_u, res_v)
            norm_next, product = two_products(res_u, res_v, image_u, image_v)
            ratio = norm_next / norm_now
            alpha = norm_next / (product - ratio * norm_next / alpha)
            dir_u = res_u + ratio * dir_u
            dir_v = res_v + ratio * dir_v
            along_u = image_u + ratio * along_u
            along_v = image_v + ratio * along_v
            norm_now = norm_next
    return (step_u, step_v)


def solution(mesh):
    placed = (P("firm", "work"), P("work", "firm"), P("work"), P("firm"), P("work"), P("firm"))
    return jax.shard_map(
        body, mesh=mesh, in_specs=placed, out_specs=(P("work"), P("firm")), check_vma=False
    )
```

profile of v0, /device:TPU:12, one launch (start us, length us, event | category | flops | bytes accessed | tf_op | source)
XLA Modules:
  0.0 947.6 jit_solution(16463058012622074813)
XLA Ops:
  0.7 29.7 %all_gather.6 = bf16[64,4096]{1,0:T(8,128)(2,1)S(1)} all-gather(bf16[8,4096]{1,0:T(8,128)(2,1)} %param.17), channel_id=1, replica_groups=mesh['work'=8,'firm'=4] {'work'}, dimensions={0}, use_global_device_ids=true | all-gather | bytes 589824 | tf_op jit(solution)/shard_map/all_gather | solution.py:12
  30.3 6.0 all_gather.7
  36.3 103.3 %while.65 = (s32[]{:T(128)}, f32[2048]{0:T(1024)S(1)}, f32[16,256]{1,0:T(8,128)S(1)}, s32[16]{0:T(128)S(1)}, bf16[64,4096]{1,0:T(8,128)(2,1)S(1)}, /*index=5*/bf...) while((s32[]{:T(128)}, f32[2048]{0:T(1024)S(1)}, ...), condition=%wide.region_1.2_spmd.clone, body=%wide.region_0.1_spmd.clone.sunk | while | flops 81793032 | bytes 6633677 | solution.py:37
  139.6 32.1 %psum.127 = f32[4096]{0:T(1024)S(1)} all-reduce(f32[4096]{0:T(1024)S(1)} %bitcast.176), channel_id=1, replica_groups=mesh['work'=8,'firm'=4] {'work'}, use_global_device_ids=true, to_apply=%region_4.5 | all-reduce | flops 4096 | bytes 32768 | tf_op jit(solution)/shard_map/psum | solution.py:42
  172.5 5.8 psum.126
  179.0 104.5 %while.66 = (s32[]{:T(128)}, f32[2048]{0:T(1024)S(1)}, f32[16,256]{1,0:T(8,128)S(1)}, s32[16]{0:T(128)S(1)}, bf16[64,4096]{1,0:T(8,128)(2,1)S(1)}, /*index=5*/bf...) while((s32[]{:T(128)}, f32[2048]{0:T(1024)S(1)}, ...), condition=%wide.region_8.9_spmd.clone, body=%wide.region_7.8_spmd.clone.sunk | while | flops 81793032 | bytes 6644961 | solution.py:37
  183.7 1.7 fusion.134
  190.3 1.7 fusion.134
  196.8 1.7 fusion.134
  203.3 1.7 fusion.134
  209.8 1.7 fusion.134
  216.4 1.7 fusion.134
  222.9 1.7 fusion.134
  229.4 1.7 fusion.134
  283.4 6.7 psum.129
  291.5 36.0 %psum.130 = f32[4096]{0:T(1024)S(1)} all-reduce(f32[4096]{0:T(1024)S(1)} %bitcast.177), channel_id=1, replica_groups=mesh['work'=8,'firm'=4] {'work'}, use_global_device_ids=true, to_apply=%region_11.12 | all-reduce | flops 4096 | bytes 32768 | tf_op jit(solution)/shard_map/psum | solution.py:42
  330.2 43.5 %all-reduce.3 = (f32[]{:T(128)}, f32[]{:T(128)}) all-reduce(f32[]{:T(128)S(6)} %add.194, f32[]{:T(128)S(6)} %add.197), channel_id=1, replica_groups=mesh['work'=8,'firm'=4] {'work','firm'}, use_global_device_ids=true, to_apply=%region_6.7 | all-reduce | flops 2 | bytes 16 | tf_op jit(solution)/shard_map/psum | solution.py:67
  375.1 101.1 %while.67 = (s32[]{:T(128)}, f32[2048]{0:T(1024)S(1)}, f32[16,256]{1,0:T(8,128)S(1)}, s32[16]{0:T(128)S(1)}, bf16[64,4096]{1,0:T(8,128)(2,1)S(1)}, /*index=5*/bf...) while((s32[]{:T(128)}, f32[2048]{0:T(1024)S(1)}, ...), condition=%wide.region_18.19_spmd.clone, body=%wide.region_17.18_spmd.clone.sunk | while | flops 81793032 | bytes 6644961 | solution.py:37
  385.9 1.7 fusion.143
  417.5 1.7 fusion.143
  476.1 5.8 psum.133
  483.1 27.5 %psum.134 = f32[4096]{0:T(1024)S(1)} all-reduce(f32[4096]{0:T(1024)S(1)} %bitcast.178), channel_id=1, replica_groups=mesh['work'=8,'firm'=4] {'work'}, use_global_device_ids=true, to_apply=%region_21.22 | all-reduce | flops 4096 | bytes 32768 | tf_op jit(solution)/shard_map/psum | solution.py:42
  513.1 46.4 %all-reduce.2 = (f32[]{:T(128)}, f32[]{:T(128)}) all-reduce(f32[]{:T(128)S(6)} %add.198, f32[]{:T(128)S(6)} %add.201), channel_id=1, replica_groups=mesh['work'=8,'firm'=4] {'work','firm'}, use_global_device_ids=true, to_apply=%region_16.17 | all-reduce | flops 2 | bytes 16 | tf_op jit(solution)/shard_map/psum | solution.py:67
  564.0 102.5 %while.68 = (s32[]{:T(128)}, f32[2048]{0:T(1024)S(1)}, f32[16,256]{1,0:T(8,128)S(1)}, s32[16]{0:T(128)S(1)}, bf16[64,4096]{1,0:T(8,128)(2,1)S(1)}, /*index=5*/bf...) while((s32[]{:T(128)}, f32[2048]{0:T(1024)S(1)}, ...), condition=%wide.region_28.29_spmd.clone, body=%wide.region_27.28_spmd.clone.sunk | while | flops 81793032 | bytes 6644961 | solution.py:37
  619.9 1.7 fusion.152
  666.5 5.8 psum.137
  673.6 27.5 %psum.138 = f32[4096]{0:T(1024)S(1)} all-reduce(f32[4096]{0:T(1024)S(1)} %bitcast.179), channel_id=1, replica_groups=mesh['work'=8,'firm'=4] {'work'}, use_global_device_ids=true, to_apply=%region_31.32 | all-reduce | flops 4096 | bytes 32768 | tf_op jit(solution)/shard_map/psum | solution.py:42
  703.8 46.4 %all-reduce.1 = (f32[]{:T(128)}, f32[]{:T(128)}) all-reduce(f32[]{:T(128)S(6)} %add.206, f32[]{:T(128)S(6)} %add.209), channel_id=1, replica_groups=mesh['work'=8,'firm'=4] {'work','firm'}, use_global_device_ids=true, to_apply=%region_26.27 | all-reduce | flops 2 | bytes 16 | tf_op jit(solution)/shard_map/psum | solution.py:67
  754.1 104.5 %while.69 = (s32[]{:T(128)}, f32[2048]{0:T(1024)S(1)}, f32[16,256]{1,0:T(8,128)S(1)}, s32[16]{0:T(128)S(1)}, bf16[64,4096]{1,0:T(8,128)(2,1)S(1)}, /*index=5*/bf...) while((s32[]{:T(128)}, f32[2048]{0:T(1024)S(1)}, ...), condition=%wide.region_38.39_spmd.clone, body=%wide.region_37.38_spmd.clone.sunk | while | flops 81793032 | bytes 6644961 | solution.py:37
  858.5 5.8 psum.141
  865.7 27.5 %psum.142 = f32[4096]{0:T(1024)S(1)} all-reduce(f32[4096]{0:T(1024)S(1)} %bitcast.180), channel_id=1, replica_groups=mesh['work'=8,'firm'=4] {'work'}, use_global_device_ids=true, to_apply=%region_41.42 | all-reduce | flops 4096 | bytes 32768 | tf_op jit(solution)/shard_map/psum | solution.py:42
  895.8 46.5 %all-reduce = (f32[]{:T(128)}, f32[]{:T(128)}) all-reduce(f32[]{:T(128)S(6)} %add.214, f32[]{:T(128)S(6)} %add.217), channel_id=1, replica_groups=mesh['work'=8,'firm'=4] {'work','firm'}, use_global_device_ids=true, to_apply=%region_36.37 | all-reduce | flops 2 | bytes 16 | tf_op jit(solution)/shard_map/psum | solution.py:67
  (655 shorter events, 449.0 us)
Async XLA Ops:
  36.3 135.4 %copy-start = (s32[4096]{0:T(1024)S(1)}, s32[4096]{0:T(1024)}, u32[]{:S(2)}) copy-start(s32[4096]{0:T(1024)} %param.21) | copy-start | bytes 49156
  36.3 141.9 %copy-start.1 = (s32[2048]{0:T(1024)S(1)}, s32[2048]{0:T(1024)}, u32[]{:S(2)}) copy-start(s32[2048]{0:T(1024)} %param.20) | copy-start | bytes 24580
where the time goes:
time: 957 us; the launch traced here: 948 us
  blocking collectives  399 us (42%)
  matrix products  340 us (36%)
  local copies, waits for them, and re-layouts  120 us (13%)
  loops' own time  55.9 us (6%)
  between operations  24.8 us (3%)
    psum x4, blocking collectives, two_products(): lax.psum((local_dot(left_u, left_v, left_u, left_v), local_dot(left_u, le...  183 us
    psum x5, blocking collectives, kernel_pass(): cols = lax.psum(cols_part, 'work')  151 us
    dot_general x80, matrix products, step(): col_blk = jnp.dot(vec_u, kernel, precision=lax.Precision.HIGHEST)  138 us
    dot_general x80, matrix products, step(): lax.dot_general(wfeat, feat_blk, (((0,), (0,)), ((), ())), preferred_elem...  106 us
    dot_general x80, matrix products, step(): jnp.dot(kernel, vec_blk, precision=lax.Precision.HIGHEST)  94.9 us
    dynamic_slice x80, local copies, waits for them, and re-layouts, step(): pot_blk = lax.dynamic_slice_in_dim(firm_pot, start, width, 0)  61.2 us
    another operation x5, loops' own time, kernel_pass(): lax.scan(step, jnp.zeros((rows_here,), jnp.float32), jnp.arange(blocks, d...  55.9 us
    dynamic_slice x80, local copies, waits for them, and re-layouts, kernel_pass(): lax.scan(step, jnp.zeros((rows_here,), jnp.float32), jnp.arange(blocks, d...  50.6 us

commit v1 on v0

--- a/solution.py
+++ b/solution.py
@@ -65,11 +65,14 @@
 
     def two_products(left_u, left_v, image_u, image_v):
         return lax.psum(
-            (
-                local_dot(left_u, left_v, left_u, left_v),
-                local_dot(left_u, left_v, image_u, image_v),
+            lax.psum(
+                (
+                    local_dot(left_u, left_v, left_u, left_v),
+                    local_dot(left_u, left_v, image_u, image_v),
+                ),
+                "firm",
             ),
-            ("work", "firm"),
+            "work",
         )
 
     image_u, image_v = hessian(res_u, res_v)

time: 957 us -> 896 us (0.936)
  blocking collectives: 399 us -> 336 us
    psum x4, blocking collectives: 183 us -> 24.8 us  [two_products(): lax.psum((local_dot(left_u, left_v, left_u, left_v), local_dot(left_u, le...]
    psum x0 -> x4, blocking collectives: none -> 84.6 us  [two_products(): lax.psum(lax.psum((local_dot(left_u, left_v, left_u, left_v), local_dot(l...]
    psum x5, blocking collectives: 151 us -> 161 us  [kernel_pass(): cols = lax.psum(cols_part, 'work')]
where the time goes in v1:
time: 896 us; the launch traced here: 883 us
  matrix products  339 us (38%)
  blocking collectives  336 us (38%)
  local copies, waits for them, and re-layouts  119 us (13%)
  loops' own time  55.2 us (6%)
  between operations  24.8 us (3%)
    psum x5, blocking collectives, kernel_pass(): cols = lax.psum(cols_part, 'work')  161 us
    dot_general x80, matrix products, step(): col_blk = jnp.dot(vec_u, kernel, precision=lax.Precision.HIGHEST)  138 us
    dot_general x80, matrix products, step(): lax.dot_general(wfeat, feat_blk, (((0,), (0,)), ((), ())), preferred_elem...  106 us
    dot_general x80, matrix products, step(): jnp.dot(kernel, vec_blk, precision=lax.Precision.HIGHEST)  94.9 us
    psum x4, blocking collectives, two_products(): lax.psum(lax.psum((local_dot(left_u, left_v, left_u, left_v), local_dot(l...  84.6 us
    dynamic_slice x80, local copies, waits for them, and re-layouts, step(): pot_blk = lax.dynamic_slice_in_dim(firm_pot, start, width, 0)  61.2 us
    another operation x5, loops' own time, kernel_pass(): lax.scan(step, jnp.zeros((rows_here,), jnp.float32), jnp.arange(blocks, d...  55.2 us
    dynamic_slice x80, local copies, waits for them, and re-layouts, kernel_pass(): lax.scan(step, jnp.zeros((rows_here,), jnp.float32), jnp.arange(blocks, d...  49.4 us

profile of v1, /device:TPU:12, one launch (start us, length us, event | category | flops | bytes accessed | tf_op | source)
XLA Modules:
  0.0 882.7 jit_solution(10881043635695293711)
XLA Ops:
  0.7 29.7 %all_gather.6 = bf16[64,4096]{1,0:T(8,128)(2,1)S(1)} all-gather(bf16[8,4096]{1,0:T(8,128)(2,1)} %param.17), channel_id=1, replica_groups=mesh['work'=8,'firm'=4] {'work'}, dimensions={0}, use_global_device_ids=true | all-gather | bytes 589824 | tf_op jit(solution)/shard_map/all_gather | solution.py:12
  30.3 6.0 all_gather.7
  36.3 103.3 %while.65 = (s32[]{:T(128)}, f32[2048]{0:T(1024)S(1)}, f32[16,256]{1,0:T(8,128)S(1)}, s32[16]{0:T(128)S(1)}, bf16[64,4096]{1,0:T(8,128)(2,1)S(1)}, /*index=5*/bf...) while((s32[]{:T(128)}, f32[2048]{0:T(1024)S(1)}, ...), condition=%wide.region_1.2_spmd.clone, body=%wide.region_0.1_spmd.clone.sunk | while | flops 81793032 | bytes 6633677 | solution.py:37
  139.6 32.1 %psum.183 = f32[4096]{0:T(1024)S(1)} all-reduce(f32[4096]{0:T(1024)S(1)} %bitcast.176), channel_id=1, replica_groups=mesh['work'=8,'firm'=4] {'work'}, use_global_device_ids=true, to_apply=%region_4.5 | all-reduce | flops 4096 | bytes 32768 | tf_op jit(solution)/shard_map/psum | solution.py:42
  172.5 5.8 psum.182
  179.0 104.5 %while.66 = (s32[]{:T(128)}, f32[2048]{0:T(1024)S(1)}, f32[16,256]{1,0:T(8,128)S(1)}, s32[16]{0:T(128)S(1)}, bf16[64,4096]{1,0:T(8,128)(2,1)S(1)}, /*index=5*/bf...) while((s32[]{:T(128)}, f32[2048]{0:T(1024)S(1)}, ...), condition=%wide.region_9.10_spmd.clone, body=%wide.region_8.9_spmd.clone.sunk | while | flops 81793032 | bytes 6644961 | solution.py:37
  183.7 1.7 fusion.134
  190.3 1.7 fusion.134
  196.8 1.7 fusion.134
  203.3 1.7 fusion.134
  209.8 1.7 fusion.134
  216.4 1.7 fusion.134
  283.4 6.7 psum.186
  291.5 36.0 %psum.187 = f32[4096]{0:T(1024)S(1)} all-reduce(f32[4096]{0:T(1024)S(1)} %bitcast.177), channel_id=1, replica_groups=mesh['work'=8,'firm'=4] {'work'}, use_global_device_ids=true, to_apply=%region_12.13 | all-reduce | flops 4096 | bytes 32768 | tf_op jit(solution)/shard_map/psum | solution.py:42
  330.2 6.2 all-reduce.7
  336.3 19.7 %all-reduce.3 = (f32[]{:T(128)}, f32[]{:T(128)}) all-reduce(f32[]{:T(128)} %get-tuple-element.552, f32[]{:T(128)} %get-tuple-element.553), channel_id=1, replica_groups=mesh['work'=8,'firm'=4] {'work'}, use_global_device_ids=true, to_apply=%region_7.8 | all-reduce | flops 2 | bytes 16 | tf_op jit(solution)/shard_map/psum | solution.py:67
  357.5 101.0 %while.67 = (s32[]{:T(128)}, f32[2048]{0:T(1024)S(1)}, f32[16,256]{1,0:T(8,128)S(1)}, s32[16]{0:T(128)S(1)}, bf16[64,4096]{1,0:T(8,128)(2,1)S(1)}, /*index=5*/bf...) while((s32[]{:T(128)}, f32[2048]{0:T(1024)S(1)}, ...), condition=%wide.region_21.22_spmd.clone, body=%wide.region_20.21_spmd.clone.sunk | while | flops 81793032 | bytes 6644961 | solution.py:37
  456.7 1.7 fusion.143
  458.5 5.8 psum.192
  465.4 31.1 %psum.193 = f32[4096]{0:T(1024)S(1)} all-reduce(f32[4096]{0:T(1024)S(1)} %bitcast.178), channel_id=1, replica_groups=mesh['work'=8,'firm'=4] {'work'}, use_global_device_ids=true, to_apply=%region_24.25 | all-reduce | flops 4096 | bytes 32768 | tf_op jit(solution)/shard_map/psum | solution.py:42
  499.0 6.2 all-reduce.6
  505.3 21.7 %all-reduce.2 = (f32[]{:T(128)}, f32[]{:T(128)}) all-reduce(f32[]{:T(128)} %get-tuple-element.550, f32[]{:T(128)} %get-tuple-element.551), channel_id=1, replica_groups=mesh['work'=8,'firm'=4] {'work'}, use_global_device_ids=true, to_apply=%region_19.20 | all-reduce | flops 2 | bytes 16 | tf_op jit(solution)/shard_map/psum | solution.py:67
  531.4 102.5 %while.68 = (s32[]{:T(128)}, f32[2048]{0:T(1024)S(1)}, f32[16,256]{1,0:T(8,128)S(1)}, s32[16]{0:T(128)S(1)}, bf16[64,4096]{1,0:T(8,128)(2,1)S(1)}, /*index=5*/bf...) while((s32[]{:T(128)}, f32[2048]{0:T(1024)S(1)}, ...), condition=%wide.region_33.34_spmd.clone, body=%wide.region_32.33_spmd.clone.sunk | while | flops 81793032 | bytes 6644961 | solution.py:37
  634.0 5.8 psum.198
  641.0 31.1 %psum.199 = f32[4096]{0:T(1024)S(1)} all-reduce(f32[4096]{0:T(1024)S(1)} %bitcast.179), channel_id=1, replica_groups=mesh['work'=8,'firm'=4] {'work'}, use_global_device_ids=true, to_apply=%region_36.37 | all-reduce | flops 4096 | bytes 32768 | tf_op jit(solution)/shard_map/psum | solution.py:42
  674.8 6.2 all-reduce.5
  680.9 21.6 %all-reduce.1 = (f32[]{:T(128)}, f32[]{:T(128)}) all-reduce(f32[]{:T(128)} %get-tuple-element.548, f32[]{:T(128)} %get-tuple-element.549), channel_id=1, replica_groups=mesh['work'=8,'firm'=4] {'work'}, use_global_device_ids=true, to_apply=%region_31.32 | all-reduce | flops 2 | bytes 16 | tf_op jit(solution)/shard_map/psum | solution.py:67
  706.6 102.5 %while.69 = (s32[]{:T(128)}, f32[2048]{0:T(1024)S(1)}, f32[16,256]{1,0:T(8,128)S(1)}, s32[16]{0:T(128)S(1)}, bf16[64,4096]{1,0:T(8,128)(2,1)S(1)}, /*index=5*/bf...) while((s32[]{:T(128)}, f32[2048]{0:T(1024)S(1)}, ...), condition=%wide.region_45.46_spmd.clone, body=%wide.region_44.45_spmd.clone.sunk | while | flops 81793032 | bytes 6644961 | solution.py:37
  809.1 5.8 psum.204
  816.2 31.1 %psum.205 = f32[4096]{0:T(1024)S(1)} all-reduce(f32[4096]{0:T(1024)S(1)} %bitcast.180), channel_id=1, replica_groups=mesh['work'=8,'firm'=4] {'work'}, use_global_device_ids=true, to_apply=%region_48.49 | all-reduce | flops 4096 | bytes 32768 | tf_op jit(solution)/shard_map/psum | solution.py:42
  849.7 6.2 all-reduce.4
  855.9 21.5 %all-reduce = (f32[]{:T(128)}, f32[]{:T(128)}) all-reduce(f32[]{:T(128)} %get-tuple-element.546, f32[]{:T(128)} %get-tuple-element.547), channel_id=1, replica_groups=mesh['work'=8,'firm'=4] {'work'}, use_global_device_ids=true, to_apply=%region_43.44 | all-reduce | flops 2 | bytes 16 | tf_op jit(solution)/shard_map/psum | solution.py:67
  (659 shorter events, 454.4 us)
Async XLA Ops:
  36.3 135.4 %copy-start = (s32[4096]{0:T(1024)S(1)}, s32[4096]{0:T(1024)}, u32[]{:S(2)}) copy-start(s32[4096]{0:T(1024)} %param.21) | copy-start | bytes 49156
  36.3 141.9 %copy-start.1 = (s32[2048]{0:T(1024)S(1)}, s32[2048]{0:T(1024)}, u32[]{:S(2)}) copy-start(s32[2048]{0:T(1024)} %param.20) | copy-start | bytes 24580
